TPU v7x, 32 devices: a whole 2x2x4 slice. The times are simulated.
32 devices in a mesh: dp: 8 (over z, x), mp: 4 (over y, core).
Axes of the slice: x: 2, y: 2, z: 4, core: 2. Of those that a mesh axis runs over, the one named last changes fastest.
Arguments:
- activations: bfloat16 [4096, 3072], P('dp', 'mp'), may hold values from -6 to 6
- out_grads: bfloat16 [4096, 6144], P('dp', 'mp'), may hold values from -0.25 to 0.25
- error: bfloat16 [8, 3072, 6144], P('dp', 'mp'), may hold values from -8 to 8
- sketch: bfloat16 [6144, 64], replicated, may hold values from -0.078125 to 0.078125
- momentum: float32 [3072, 6144], P('mp', 'dp'), may hold values from -6 to 6
Outputs:
- error_new: bfloat16 [8, 3072, 6144], P('dp', 'mp')
- momentum_new: float32 [3072, 6144], P('mp', 'dp')
- next_sketch: bfloat16 [6144, 64], replicated
All inputs are finite; a program needn't handle non-finite values.
Results may differ from a plain program's by a relative error of at most 0.0057.
Values may be sent and summed in bfloat16 or wider, within the bound.
A program may use at most 64 MiB of HBM per device.

v0:
```python
import jax
import jax.numpy as jnp
from jax import lax
from jax.sharding import PartitionSpec as P

beta_decay = 0.9


def update_momentum(momentum, basis_rows, sketch_block):
    product = lax.dot_general(
        basis_rows, sketch_block, (((1,), (1,)), ((), ())), preferred_element_type=jnp.float32
    )
    return beta_decay * momentum + product


def local(activations, out_grads, error, sketch, momentum):
    own_error = error[0]
    product = lax.dot_general(
        activations,
        lax.all_gather(out_grads, "mp", axis=1, tiled=True),
        (((0,), (0,)), ((), ())),
        preferred_element_type=jnp.float32,
    )
    accumulated = (product + own_error.astype(jnp.float32)).astype(jnp.bfloat16)
    local_left = jnp.dot(accumulated, sketch, preferred_element_type=jnp.float32)
    left_sketch = lax.psum(local_left, "dp")
    gram_local = jnp.dot(
        left_sketch.T,
        left_sketch,
        precision=lax.Precision.HIGHEST,
        preferred_element_type=jnp.float32,
    )
    gram_matrix = lax.psum(gram_local, "mp")
    factor = jnp.linalg.cholesky(gram_matrix)
    basis_rows = jax.scipy.linalg.solve_triangular(factor, left_sketch.T, lower=True).T.astype(
        jnp.bfloat16
    )
    block_width = momentum.shape[1]
    local_right = lax.dot_general(
        accumulated, basis_rows, (((0,), (0,)), ((), ())), preferred_element_type=jnp.float32
    )
    right_sketch = lax.psum(local_right, ("dp", "mp"))
    next_sketch = right_sketch.astype(jnp.bfloat16)
    sketch_part = lax.dynamic_slice_in_dim(
        next_sketch, lax.axis_index("dp") * block_width, block_width, 0
    )
    momentum_new = update_momentum(momentum, basis_rows, sketch_part)
    decoded = lax.dot_general(
        basis_rows, next_sketch, (((1,), (1,)), ((), ())), preferred_element_type=jnp.float32
    )
    error_new = (accumulated.astype(jnp.float32) - decoded / lax.axis_size("dp")).astype(
        jnp.bfloat16
    )
    return (error_new[None], momentum_new, next_sketch)


def solution(mesh):
    in_specs = (P("dp", "mp"), P("dp", "mp"), P("dp", "mp", None), P(), P("mp", "dp"))
    out_specs = (P("dp", "mp", None), P("mp", "dp"), P())
    return jax.shard_map(local, mesh=mesh, in_specs=in_specs, out_specs=out_specs, check_vma=False)
```

profile of v0, /device:TPU:0, one launch (start us, length us, event | category | flops | bytes accessed | tf_op | source)
XLA Modules:
  0.0 249.4 jit_solution(14047941913646381180)
XLA Ops:
  7.2 0.0 copy-start
  7.2 0.0 all-gather.2.cloned.1.call-start
  7.2 0.7 all-gather.2.cloned.1.call-update
  7.9 0.0 copy-start.4
  7.9 0.0 all-reduce.3.cloned.1.call-start
  8.0 50.7 %all-gather.2.cloned.1.call-done = bf16[512,6144]{1,0:T(8,128)(2,1)} async-done(((bf16[512,1536]{1,0:T(8,128)(2,1)}), bf16[512,6144]{1,0:T(8,128)(2,1)}) %all-gather.2.cloned.1.call-update) | async-done | bytes 6291472 | tf_op jit(solution)/shard_map/all_gather | solution.py:20
  58.7 0.0 copy-done
  58.7 9.6 %fusion = bf16[768,6144]{1,0:T(8,128)(2,1)S(1)} fusion(bf16[1,768,6144]{2,1,0:T(8,128)(2,1)} %param.7, bf16[512,768]{1,0:T(8,128)(2,1)S(1)} %copy-done, bf16[512,6144]{1,0:T(8,128)(2,1)} %all-gather.2.cloned.1.call-done), kind=kOutput, calls=%fused_computation.1 | convolution fusion | flops 4845993984 | bytes 25952256 | tf_op jit(solution)/shard_map/dot_general | solution.py:18
  68.3 0.0 copy-start.1
  68.3 3.7 %copy-done.1 = bf16[768,6144]{1,0:T(8,128)(2,1)} copy-done((bf16[768,6144]{1,0:T(8,128)(2,1)}, bf16[768,6144]{1,0:T(8,128)(2,1)S(1)}, u32[]{:S(2)}) %copy-start.1) | copy-done | bytes 9437208
  72.1 0.0 copy-done.4
  72.1 3.7 %fusion.7 = f32[768,64]{0,1:T(8,128)} fusion(bf16[768,6144]{1,0:T(8,128)(2,1)S(1)} %fusion, bf16[6144,64]{0,1:T(8,128)(2,1)S(1)} %copy-done.4), kind=kOutput, calls=%fused_computation.17 | convolution fusion | flops 603979776 | bytes 10420224 | tf_op jit(solution)/shard_map/dot_general | solution.py:25
  75.7 0.0 all-reduce.3.cloned.1.call-update
  75.8 70.8 %all-reduce.3.cloned.1.call-done = f32[768,64]{0,1:T(8,128)} async-done(((f32[768,64]{0,1:T(8,128)}), f32[768,64]{0,1:T(8,128)}) %all-reduce.3.cloned.1.call-update) | async-done | bytes 196624 | tf_op jit(solution)/shard_map/psum | solution.py:26
  146.6 1.3 fusion.8
  147.9 10.3 %psum.22 = f32[64,64]{0,1:T(8,128)S(1)} all-reduce(f32[64,64]{0,1:T(8,128)S(1)} %fusion.8), channel_id=1, replica_groups=mesh['dp'=8,'mp'=4] {'mp'}, use_global_device_ids=true, to_apply=%region_1.0 | all-reduce | flops 4096 | bytes 32768 | tf_op jit(solution)/shard_map/psum | solution.py:33
  158.2 0.1 copy.9
  158.3 5.8 %cholesky.16 = f32[64,64]{1,0:T(8,128)S(1)} custom-call(f32[64,64]{1,0:T(8,128)S(1)} %fusion.5), custom_call_target="Cholesky" | custom-call | tf_op jit(solution)/shard_map/jit(cholesky)/cholesky | solution.py:34
  164.2 0.6 compare_reduce_fusion
  164.8 0.7 fusion.3
  165.5 4.9 %custom-call.7 = f32[1,64,64]{1,2,0:T(8,128)S(1)} custom-call(f32[1,64,64]{2,1,0:T(8,128)S(1)} %fusion.3), custom_call_target="InvertDiagBlocksLowerTriangular" | custom-call | tf_op jit(solution)/shard_map/jit(_solve_triangular)/triangular_solve | solution.py:35
  170.4 1.3 convolution_convert_fusion
  171.7 5.4 %fusion.9 = f32[6144,64]{0,1:T(8,128)S(1)} fusion(bf16[768,64]{0,1:T(8,128)(2,1)S(1)} %convolution_convert_fusion, bf16[768,6144]{1,0:T(8,128)(2,1)} %copy-done.1), kind=kOutput, calls=%fused_computation.19 | convolution fusion | flops 603979776 | bytes 11108352 | tf_op jit(solution)/shard_map/dot_general | solution.py:39
  177.1 55.7 %all-reduce.4 = bf16[6144,64]{0,1:T(8,128)(2,1)S(1)} all-reduce(f32[6144,64]{0,1:T(8,128)S(1)} %fusion.9), channel_id=1, replica_groups=mesh['dp'=8,'mp'=4] {'dp','mp'}, use_global_device_ids=true, to_apply=%region_4.5 | all-reduce | flops 393216 | bytes 2359296 | tf_op jit(solution)/shard_map/psum | solution.py:42
  232.8 0.0 copy-start.2
  232.8 0.0 copy-start.3
  232.8 7.8 %fusion.1 = bf16[1,768,6144]{2,1,0:T(8,128)(2,1)} fusion(bf16[768,64]{0,1:T(8,128)(2,1)S(1)} %convolution_convert_fusion, bf16[6144,64]{0,1:T(8,128)(2,1)S(1)} %all-reduce.4, bf16[768,6144]{1,0:T(8,128)(2,1)} %copy-done.1), kind=kOutput, calls=%fused_computation.3 | convolution fusion | flops 622854144 | bytes 19759104 | tf_op jit(solution)/shard_map/dot_general | solution.py:48
  240.7 0.0 copy-done.2
  240.7 0.0 copy-done.3
  240.7 1.9 multiply_add_fusion
  (2 shorter events, 0.0 us)
Async XLA Ops:
  7.2 51.5 %copy-start = (bf16[512,768]{1,0:T(8,128)(2,1)S(1)}, bf16[512,768]{1,0:T(8,128)(2,1)}, u32[]{:S(2)}) copy-start(bf16[512,768]{1,0:T(8,128)(2,1)} %param.5) | copy-start | bytes 2359300
  7.2 51.5 %all-gather.2.cloned.1.call-start = ((), (), s32[]{:S(2)}) async-start(), calls=%async_computation | async-start | bytes 7864320 | tf_op jit(solution)/shard_map/all_gather | solution.py:20
  7.9 64.2 %copy-start.4 = (bf16[6144,64]{0,1:T(8,128)(2,1)S(1)}, bf16[6144,64]{0,1:T(8,128)(2,1)}, u32[]{:S(2)}) copy-start(bf16[6144,64]{0,1:T(8,128)(2,1)} %param.8) | copy-start | bytes 2359300
  7.9 138.7 %all-reduce.3.cloned.1.call-start = ((), (), s32[]{:S(2)}) async-start(), calls=%async_computation.1 | async-start | bytes 393216 | tf_op jit(solution)/shard_map/psum | solution.py:26
  68.3 3.7 %copy-start.1 = (bf16[768,6144]{1,0:T(8,128)(2,1)}, bf16[768,6144]{1,0:T(8,128)(2,1)S(1)}, u32[]{:S(2)}) copy-start(bf16[768,6144]{1,0:T(8,128)(2,1)S(1)} %fusion) | copy-start | bytes 28311556
  232.8 7.8 %copy-start.2 = (bf16[6144,64]{0,1:T(8,128)(2,1)}, bf16[6144,64]{0,1:T(8,128)(2,1)S(1)}, u32[]{:S(2)}) copy-start(bf16[6144,64]{0,1:T(8,128)(2,1)S(1)} %all-reduce.4) | copy-start | bytes 2359300
  232.8 7.8 %copy-start.3 = (f32[768,768]{1,0:T(8,128)S(1)}, f32[768,768]{1,0:T(8,128)}, u32[]{:S(2)}) copy-start(f32[768,768]{1,0:T(8,128)} %param.9) | copy-start | bytes 7077892
Sparse Core Ops, SparseCore 0:
  9.5 49.0 all-gather.1
  75.9 70.6 all-reduce.2
where the time goes:
time: 250 us; the launch traced here: 249 us
  waiting for transfers between devices  122 us (49%)
  blocking collectives  66 us (26%)
  matrix products  31.1 us (12%)
  between operations  14.2 us (6%)
  other arithmetic  12.1 us (5%)
  local copies, waits for them, and re-layouts  3.84 us (2%)
    psum x1, waiting for transfers between devices, local(): left_sketch = lax.psum(local_left, 'dp')  70.8 us
    psum x1, blocking collectives, local(): right_sketch = lax.psum(local_right, ('dp', 'mp'))  55.7 us
    all_gather x1, waiting for transfers between devices, local(): lax.all_gather(out_grads, 'mp', axis=1, tiled=True)  50.7 us
    psum x1, blocking collectives, local(): gram_matrix = lax.psum(gram_local, 'mp')  10.3 us
    dot_general x1, matrix products, local(): lax.dot_general(activations, lax.all_gather(out_grads, 'mp', axis=1, tile...  9.64 us
    dot_general x1, matrix products, local(): lax.dot_general(basis_rows, next_sketch, (((1,), (1,)), ((), ())), prefer...  7.81 us
    another operation x3, other arithmetic, local(): factor = jnp.linalg.cholesky(gram_matrix)  6.52 us
    another operation x2, other arithmetic, local(): jax.scipy.linalg.solve_triangular(factor, left_sketch.T, lower=True)  5.55 us
  transfers between devices with their start and end apart: 2, of which 2 were waited for; matrix products, arithmetic and copies ran while one was open for 0% of the time, Pallas kernels for 0%

commit v1 on v0

--- a/solution.py
+++ b/solution.py
@@ -23,7 +23,8 @@
     )
     accumulated = (product + own_error.astype(jnp.float32)).astype(jnp.bfloat16)
     local_left = jnp.dot(accumulated, sketch, preferred_element_type=jnp.float32)
-    left_sketch = lax.psum(local_left, "dp")
+    wait_edges_now = lambda local_x: jnp.sum(lax.all_gather(local_x, "dp"), axis=0)
+    left_sketch = wait_edges_now(local_left)
     gram_local = jnp.dot(
         left_sketch.T,
         left_sketch,

time: 250 us -> 224 us (0.90)
  waiting for transfers between devices: 122 us -> 95.7 us
    psum x1 -> x0, waiting for transfers between devices: 70.8 us -> none  [local(): left_sketch = lax.psum(local_left, 'dp')]
    all_gather x0 -> x1, waiting for transfers between devices: none -> 44.3 us  [local(): lax.all_gather(local_x, 'dp')]
    unnamed x10 -> x11, local copies, waits for them, and re-layouts: 3.76 us -> 5.64 us
where the time goes in v1:
time: 224 us
  waiting for transfers between devices  95.7 us (43%)
  blocking collectives  66.5 us (30%)
  matrix products  29.1 us (13%)
  between operations  14.2 us (6%)
  other arithmetic  12.5 us (6%)
  local copies, waits for them, and re-layouts  5.72 us (3%)
    psum x1, blocking collectives, local(): right_sketch = lax.psum(local_right, ('dp', 'mp'))  56.2 us
    all_gather x1, waiting for transfers between devices, local(): lax.all_gather(out_grads, 'mp', axis=1, tiled=True)  50.7 us
    all_gather x1, waiting for transfers between devices, local(): lax.all_gather(local_x, 'dp')  44.3 us
    psum x1, blocking collectives, local(): gram_matrix = lax.psum(gram_local, 'mp')  10.3 us
    dot_general x1, matrix products, local(): lax.dot_general(activations, lax.all_gather(out_grads, 'mp', axis=1, tile...  9.64 us
    dot_general x1, matrix products, local(): lax.dot_general(basis_rows, next_sketch, (((1,), (1,)), ((), ())), prefer...  7.82 us
    another operation x3, other arithmetic, local(): factor = jnp.linalg.cholesky(gram_matrix)  6.52 us
    unnamed x11, local copies, waits for them, and re-layouts  5.64 us
  transfers between devices with their start and end apart: 2, of which 2 were waited for; matrix products, arithmetic and copies ran while one was open for 0% of the time, Pallas kernels for 0%

profile of v1, /device:TPU:0, one launch (start us, length us, event | category | flops | bytes accessed | tf_op | source)
XLA Modules:
  0.0 223.8 jit_solution(8009464143487280420)
XLA Ops:
  7.2 0.0 copy-start
  7.2 0.0 all-gather.4.cloned.1.call-start
  7.2 0.7 all-gather.4.cloned.1.call-update
  7.9 0.0 copy-start.4
  7.9 0.0 all-gather.6.cloned.1.call-start
  8.0 50.7 %all-gather.4.cloned.1.call-done = bf16[512,6144]{1,0:T(8,128)(2,1)} async-done(((bf16[512,1536]{1,0:T(8,128)(2,1)}), bf16[512,6144]{1,0:T(8,128)(2,1)}) %all-gather.4.cloned.1.call-update) | async-done | bytes 6291472 | tf_op jit(solution)/shard_map/all_gather | solution.py:20
  58.7 0.0 copy-done
  58.7 9.6 %fusion = bf16[768,6144]{1,0:T(8,128)(2,1)S(1)} fusion(bf16[1,768,6144]{2,1,0:T(8,128)(2,1)} %param.7, bf16[512,768]{1,0:T(8,128)(2,1)S(1)} %copy-done, bf16[512,6144]{1,0:T(8,128)(2,1)} %all-gather.4.cloned.1.call-done), kind=kOutput, calls=%fused_computation.1 | convolution fusion | flops 4845993984 | bytes 25952256 | tf_op jit(solution)/shard_map/dot_general | solution.py:18
  68.3 0.0 copy-start.1
  68.3 3.7 %copy-done.1 = bf16[768,6144]{1,0:T(8,128)(2,1)} copy-done((bf16[768,6144]{1,0:T(8,128)(2,1)}, bf16[768,6144]{1,0:T(8,128)(2,1)S(1)}, u32[]{:S(2)}) %copy-start.1) | copy-done | bytes 9437208
  72.1 0.0 copy-done.4
  72.1 3.7 %fusion.7 = f32[768,64]{0,1:T(8,128)} fusion(bf16[768,6144]{1,0:T(8,128)(2,1)S(1)} %fusion, bf16[6144,64]{0,1:T(8,128)(2,1)S(1)} %copy-done.4), kind=kOutput, calls=%fused_computation.18 | convolution fusion | flops 603979776 | bytes 10420224 | tf_op jit(solution)/shard_map/dot_general | solution.py:25
  75.7 0.0 all-gather.6.cloned.1.call-update
  75.7 44.3 %all-gather.6.cloned.1.call-done = f32[6144,64]{0,1:T(8,128)} async-done(((f32[768,64]{0,1:T(8,128)}), f32[6144,64]{0,1:T(8,128)}) %all-gather.6.cloned.1.call-update) | async-done | bytes 1572880 | tf_op jit(solution)/shard_map/all_gather | solution.py:26
  120.1 1.9 copy.13
  122.0 0.4 bitcast_reduce_fusion
  122.4 0.3 fusion.8
  122.7 10.3 %psum.14 = f32[64,64]{0,1:T(8,128)S(1)} all-reduce(f32[64,64]{0,1:T(8,128)S(1)} %fusion.8), channel_id=1, replica_groups=mesh['dp'=8,'mp'=4] {'mp'}, use_global_device_ids=true, to_apply=%region_1.0 | all-reduce | flops 4096 | bytes 32768 | tf_op jit(solution)/shard_map/psum | solution.py:34
  133.0 0.1 copy.11
  133.0 5.8 %cholesky.16 = f32[64,64]{1,0:T(8,128)S(1)} custom-call(f32[64,64]{1,0:T(8,128)S(1)} %fusion.5), custom_call_target="Cholesky" | custom-call | tf_op jit(solution)/shard_map/jit(cholesky)/cholesky | solution.py:35
  138.9 0.6 compare_reduce_fusion
  139.6 0.7 fusion.3
  140.2 4.9 %custom-call.7 = f32[1,64,64]{1,2,0:T(8,128)S(1)} custom-call(f32[1,64,64]{2,1,0:T(8,128)S(1)} %fusion.3), custom_call_target="InvertDiagBlocksLowerTriangular" | custom-call | tf_op jit(solution)/shard_map/jit(_solve_triangular)/triangular_solve | solution.py:36
  145.1 0.4 convolution_convert_fusion
  145.5 5.4 %fusion.9 = f32[6144,64]{0,1:T(8,128)S(1)} fusion(bf16[768,64]{0,1:T(8,128)(2,1)S(1)} %convolution_convert_fusion, bf16[768,6144]{1,0:T(8,128)(2,1)} %copy-done.1), kind=kOutput, calls=%fused_computation.20 | convolution fusion | flops 603979776 | bytes 11108352 | tf_op jit(solution)/shard_map/dot_general | solution.py:40
  151.0 56.2 %all-reduce.1 = bf16[6144,64]{0,1:T(8,128)(2,1)S(1)} all-reduce(f32[6144,64]{0,1:T(8,128)S(1)} %fusion.9), channel_id=1, replica_groups=mesh['dp'=8,'mp'=4] {'dp','mp'}, use_global_device_ids=true, to_apply=%region_4.5 | all-reduce | flops 393216 | bytes 2359296 | tf_op jit(solution)/shard_map/psum | solution.py:43
  207.2 0.0 copy-start.2
  207.2 0.0 copy-start.3
  207.2 7.8 %fusion.1 = bf16[1,768,6144]{2,1,0:T(8,128)(2,1)} fusion(bf16[768,64]{0,1:T(8,128)(2,1)S(1)} %convolution_convert_fusion, bf16[6144,64]{0,1:T(8,128)(2,1)S(1)} %all-reduce.1, bf16[768,6144]{1,0:T(8,128)(2,1)} %copy-done.1), kind=kOutput, calls=%fused_computation.3 | convolution fusion | flops 622854144 | bytes 19759104 | tf_op jit(solution)/shard_map/dot_general | solution.py:49
  215.0 0.0 copy-done.2
  215.0 0.0 copy-done.3
  215.0 1.9 multiply_add_fusion
  (2 shorter events, 0.0 us)
Async XLA Ops:
  7.2 51.5 %copy-start = (bf16[512,768]{1,0:T(8,128)(2,1)S(1)}, bf16[512,768]{1,0:T(8,128)(2,1)}, u32[]{:S(2)}) copy-start(bf16[512,768]{1,0:T(8,128)(2,1)} %param.5) | copy-start | bytes 2359300
  7.2 51.5 %all-gather.4.cloned.1.call-start = ((), (), s32[]{:S(2)}) async-start(), calls=%async_computation | async-start | bytes 7864320 | tf_op jit(solution)/shard_map/all_gather | solution.py:20
  7.9 64.2 %copy-start.4 = (bf16[6144,64]{0,1:T(8,128)(2,1)S(1)}, bf16[6144,64]{0,1:T(8,128)(2,1)}, u32[]{:S(2)}) copy-start(bf16[6144,64]{0,1:T(8,128)(2,1)} %param.8) | copy-start | bytes 2359300
  7.9 112.2 %all-gather.6.cloned.1.call-start = ((), (), s32[]{:S(2)}) async-start(), calls=%async_computation.1 | async-start | bytes 1769472 | tf_op jit(solution)/shard_map/all_gather | solution.py:26
  68.3 3.7 %copy-start.1 = (bf16[768,6144]{1,0:T(8,128)(2,1)}, bf16[768,6144]{1,0:T(8,128)(2,1)S(1)}, u32[]{:S(2)}) copy-start(bf16[768,6144]{1,0:T(8,128)(2,1)S(1)} %fusion) | copy-start | bytes 28311556
  207.2 7.8 %copy-start.2 = (bf16[6144,64]{0,1:T(8,128)(2,1)}, bf16[6144,64]{0,1:T(8,128)(2,1)S(1)}, u32[]{:S(2)}) copy-start(bf16[6144,64]{0,1:T(8,128)(2,1)S(1)} %all-reduce.1) | copy-start | bytes 2359300
  207.2 7.8 %copy-start.3 = (f32[768,768]{1,0:T(8,128)S(1)}, f32[768,768]{1,0:T(8,128)}, u32[]{:S(2)}) copy-start(f32[768,768]{1,0:T(8,128)} %param.9) | copy-start | bytes 7077892
Sparse Core Ops, SparseCore 0:
  9.5 49.0 all-gather.3
  75.9 44.1 all-gather.5
